TPU v7x, 128 devices: a whole 4x4x4 slice. The times are simulated.
128 devices in a mesh: seq: 16 (over z_lo, x, core), res: 8 (over y, z_hi).
Axes of the slice: x: 4, y: 4, z: 4 (z_hi: 2, z_lo: 2; z = z_hi * 2 + z_lo), core: 2. Of those that a mesh axis runs over, the one named last changes fastest.
Arguments:
- states: bfloat16 [512, 256, 768], P('seq', 'res'), may hold values from -6 to 6
- row_query: bfloat16 [768, 768], replicated, as said below
- row_key: bfloat16 [768, 768], replicated
- row_value: bfloat16 [768, 768], replicated, may hold values from -0.21875 to 0.21875
- row_out: bfloat16 [768, 768], replicated, may hold values from -0.21875 to 0.21875
- col_query: bfloat16 [768, 768], replicated, as said below
- col_key: bfloat16 [768, 768], replicated
- col_value: bfloat16 [768, 768], replicated, may hold values from -0.21875 to 0.21875
- col_out: bfloat16 [768, 768], replicated, may hold values from -0.21875 to 0.21875
Outputs:
- updated: bfloat16 [512, 256, 768], P('seq', 'res')
Inputs may be any that keep to these rules, and one draw needn't show every extreme that they name: No bound on the size of row_query and row_key entries or of the scores they give is promised. No bound on the size of col_query and col_key entries or of the scores they give is promised.
All inputs are finite; a program needn't handle non-finite values.
Results may differ from a plain program's by a relative error of at most 0.02.
Values may be sent and summed in bfloat16 or wider, within the bound.
A program may use at most 128 MiB of HBM per device.

v0:
```python
import math
import jax
import jax.numpy as jnp
from jax import lax
from jax.sharding import PartitionSpec as P

D = 768
HEADS = 12


def normalize(states):
    values = states.astype(jnp.float32)
    center = values - jnp.mean(values, axis=-1, keepdims=True)
    spread = jnp.mean(center * center, axis=-1, keepdims=True)
    return (center * lax.rsqrt(spread + 1e-05)).astype(jnp.bfloat16)


def project(inputs, weight):
    return jnp.dot(inputs, weight, preferred_element_type=jnp.float32)


def split_heads(field):
    return field.reshape(field.shape[0], field.shape[1], HEADS, D // HEADS)


def on_device(
    states, row_query, row_key, row_value, row_out, col_query, col_key, col_value, col_out
):
    row_count, col_count = (states.shape[0], states.shape[1])
    head_dim = D // HEADS
    all_rows = row_count * lax.axis_size("seq")
    tied_scale = head_dim ** (-0.5) / math.sqrt(all_rows)
    normed = normalize(states)
    q1 = project(normed, row_query).astype(jnp.bfloat16)
    k1 = project(normed, row_key).astype(jnp.bfloat16)
    v1 = project(normed, row_value).astype(jnp.bfloat16)
    q_moved, k_moved, v_moved = (
        lax.all_to_all(q1, "res", split_axis=0, concat_axis=1, tiled=True),
        lax.all_to_all(k1, "res", split_axis=0, concat_axis=1, tiled=True),
        lax.all_to_all(v1, "res", split_axis=0, concat_axis=1, tiled=True),
    )
    partial_value = (
        jnp.einsum(
            "rihd,rjhd->hij",
            split_heads(q_moved),
            split_heads(k_moved),
            preferred_element_type=jnp.float32,
        )
        * tied_scale
    )
    tied = lax.psum(partial_value, ("seq", "res"))
    prob1 = jax.nn.softmax(tied, axis=-1).astype(jnp.bfloat16)
    o_moved = jnp.einsum(
        "hij,rjhd->rihd", prob1, split_heads(v_moved), preferred_element_type=jnp.float32
    ).astype(jnp.bfloat16)
    o_moved = o_moved.reshape(o_moved.shape[0], o_moved.shape[1], D)
    o1 = lax.all_to_all(o_moved, "res", split_axis=1, concat_axis=0, tiled=True)
    mid = (states.astype(jnp.float32) + project(o1, row_out)).astype(jnp.bfloat16)
    normed2 = normalize(mid)
    q2 = project(normed2, col_query).astype(jnp.bfloat16)
    k2 = project(normed2, col_key).astype(jnp.bfloat16)
    v2 = project(normed2, col_value).astype(jnp.bfloat16)
    q_cols, k_cols, v_cols = (
        lax.all_to_all(q2, "seq", split_axis=1, concat_axis=0, tiled=True),
        lax.all_to_all(k2, "seq", split_axis=1, concat_axis=0, tiled=True),
        lax.all_to_all(v2, "seq", split_axis=1, concat_axis=0, tiled=True),
    )
    gathered_rows, local_cols = (q_cols.shape[0], q_cols.shape[1])

    def arrange(field):
        return field.reshape(gathered_rows, local_cols, HEADS, head_dim).transpose(1, 0, 2, 3)

    def attend(triple):
        query_col, key_col, value_col = triple
        score = jnp.einsum(
            "rhd,shd->hrs", query_col, key_col, preferred_element_type=jnp.float32
        ) * head_dim ** (-0.5)
        prob2 = jax.nn.softmax(score, axis=-1).astype(jnp.bfloat16)
        return jnp.einsum(
            "hrs,shd->rhd", prob2, value_col, preferred_element_type=jnp.float32
        ).astype(jnp.bfloat16)

    o2 = lax.map(attend, (arrange(q_cols), arrange(k_cols), arrange(v_cols)))
    o2 = o2.reshape(local_cols, gathered_rows, D).transpose(1, 0, 2)
    colupd = project(o2, col_out).astype(jnp.bfloat16)
    colupd = lax.all_to_all(colupd, "seq", split_axis=0, concat_axis=1, tiled=True)
    return (mid.astype(jnp.float32) + colupd.astype(jnp.float32)).astype(jnp.bfloat16)


def solution(mesh):
    placed = (P("seq", "res", None), P(), P(), P(), P(), P(), P(), P(), P())
    return jax.shard_map(
        on_device, mesh=mesh, in_specs=placed, out_specs=P("seq", "res", None), check_vma=False
    )
```

profile of v0, /device:TPU:1, one launch (start us, length us, event | category | flops | bytes accessed | tf_op | source)
XLA Modules:
  0.0 487.7 jit_solution(7350773890253013936)
XLA Ops:
  11.7 8.3 %all-to-all-start.1 = ((bf16[32,32,768]{2,1,0:T(8,128)(2,1)}), bf16[32,32,768]{2,1,0:T(8,128)(2,1)}, u32[]{:S(2)}, u32[]{:S(2)}) async-start(bf16[32,32,768]{2,1,0:T(8,128)(2,1)} %convolution_convert_fusion.5), calls=%async_computation.1 | async-start | bytes 3145728 | tf_op jit(solution)/shard_map/all_to_all | solution.py:38
  20.1 3.9 convolution_convert_fusion.4
  23.9 19.3 %all-to-all-done.1 = bf16[32,32,768]{2,1,0:T(8,128)(2,1)} async-done(((bf16[32,32,768]{2,1,0:T(8,128)(2,1)}), bf16[32,32,768]{2,1,0:T(8,128)(2,1)}, u32[]{:S(2)}, u32[]{:S(2)}) %all-to-all-start.1) | async-done | bytes 1572896 | tf_op jit(solution)/shard_map/all_to_all | solution.py:38
  43.2 4.3 all-to-all-start.2
  50.3 5.9 %reshape.63 = bf16[4,256,12,64]{3,2,1,0:T(8,128)(2,1)} reshape(bf16[4,8,32,768]{3,2,1,0:T(8,128)(2,1)} %bitcast.147) | data formatting | bytes 3145728 | tf_op jit(solution)/shard_map/reshape | solution.py:23
  56.2 13.5 %all-to-all-done.2 = bf16[32,32,768]{2,1,0:T(8,128)(2,1)} async-done(((bf16[32,32,768]{2,1,0:T(8,128)(2,1)}), bf16[32,32,768]{2,1,0:T(8,128)(2,1)}, u32[]{:S(2)}, u32[]{:S(2)}) %all-to-all-start.2) | async-done | bytes 1572896 | tf_op jit(solution)/shard_map/all_to_all | solution.py:39
  72.3 5.9 %reshape.64 = bf16[4,256,12,64]{3,2,1,0:T(8,128)(2,1)} reshape(bf16[4,8,32,768]{3,2,1,0:T(8,128)(2,1)} %bitcast.148) | data formatting | bytes 3145728 | tf_op jit(solution)/shard_map/reshape | solution.py:23
  78.2 6.7 %bitcast_multiply_fusion = f32[12,256,256]{2,1,0:T(8,128)} fusion(bf16[4,256,12,64]{3,2,1,0:T(8,128)(2,1)} %reshape.64, bf16[4,256,12,64]{3,2,1,0:T(8,128)(2,1)} %reshape.63), kind=kOutput, calls=%fused_computation.43 | convolution fusion | flops 403439616 | bytes 6291456 | tf_op jit(solution)/shard_map/rihd,rjhd->hij/dot_general | solution.py:43
  87.7 26.8 %all_to_all.117 = bf16[32,32,768]{2,1,0:T(8,128)(2,1)S(1)} all-to-all(bf16[32,32,768]{2,1,0:T(8,128)(2,1)S(1)} %convolution_convert_fusion.6), channel_id=1, replica_groups=mesh['seq'=16,'res'=8] {'res'}, dimensions={0} | all-to-all | bytes 3145728 | tf_op jit(solution)/shard_map/all_to_all | solution.py:40
  115.8 5.9 %reshape.62 = bf16[4,256,12,64]{3,2,1,0:T(8,128)(2,1)} reshape(bf16[4,8,32,768]{3,2,1,0:T(8,128)(2,1)} %bitcast.149) | data formatting | bytes 3145728 | tf_op jit(solution)/shard_map/reshape | solution.py:23
  121.7 123.8 %all-reduce.2.cloned.1.call-done = f32[12,256,256]{2,1,0:T(8,128)} async-done(((f32[12,256,256]{2,1,0:T(8,128)}), f32[12,256,256]{2,1,0:T(8,128)}) %all-reduce.2.cloned.1.call-update) | async-done | bytes 3145744 | tf_op jit(solution)/shard_map/psum | solution.py:51
  245.5 3.8 fusion.92
  249.3 12.5 %fusion.63 = bf16[4,256,12,64]{1,3,0,2:T(8,128)(2,1)} fusion(f32[12,256]{1,0:T(8,128)S(1)} %fusion.92, bf16[4,256,12,64]{3,2,1,0:T(8,128)(2,1)} %reshape.62, f32[12,256,256]{2,1,0:T(8,128)} %all-reduce.2.cloned.1.call-done), kind=kOutput, calls=%fused_computation.68 | convolution fusion | flops 405802240 | bytes 6303744 | tf_op jit(solution)/shard_map/hij,rjhd->rihd/dot_general | solution.py:53
  268.2 25.9 %all_to_all.118 = bf16[4,256,768]{2,0,1:T(4,128)(2,1)S(1)} all-to-all(bf16[4,256,768]{2,0,1:T(4,128)(2,1)} %copy.42), channel_id=1, replica_groups=mesh['seq'=16,'res'=8] {'res'}, dimensions={1} | all-to-all | bytes 3145728 | tf_op jit(solution)/shard_map/all_to_all | solution.py:57
  301.3 6.3 %all-to-all-start.6 = ((bf16[32,32,768]{2,0,1:T(8,128)(2,1)}), bf16[32,32,768]{2,0,1:T(8,128)(2,1)S(1)}, u32[]{:S(2)}, u32[]{:S(2)}) async-start(bf16[32,32,768]{2,0,1:T(8,128)(2,1)} %copy.49), calls=%async_computation.6 | async-start | bytes 3145728 | tf_op jit(solution)/shard_map/all_to_all | solution.py:65
  312.9 16.3 %all-to-all-done.6 = bf16[32,32,768]{2,0,1:T(8,128)(2,1)S(1)} async-done(((bf16[32,32,768]{2,0,1:T(8,128)(2,1)}), bf16[32,32,768]{2,0,1:T(8,128)(2,1)S(1)}, u32[]{:S(2)}, u32[]{:S(2)}) %all-to-all-start.6) | async-done | bytes 1572896 | tf_op jit(solution)/shard_map/all_to_all | solution.py:65
  329.1 4.9 all-to-all-start.5
  339.3 16.4 %all-to-all-done.5 = bf16[32,32,768]{2,0,1:T(8,128)(2,1)} async-done(((bf16[32,32,768]{2,0,1:T(8,128)(2,1)}), bf16[32,32,768]{2,0,1:T(8,128)(2,1)}, u32[]{:S(2)}, u32[]{:S(2)}) %all-to-all-start.5) | async-done | bytes 1572896 | tf_op jit(solution)/shard_map/all_to_all | solution.py:64
  355.7 13.4 %all-to-all-start.4 = ((bf16[32,32,768]{2,0,1:T(8,128)(2,1)}), bf16[32,32,768]{2,0,1:T(8,128)(2,1)}, u32[]{:S(2)}, u32[]{:S(2)}) async-start(bf16[32,32,768]{2,0,1:T(8,128)(2,1)} %copy.45), calls=%async_computation.4 | async-start | bytes 3145728 | tf_op jit(solution)/shard_map/all_to_all | solution.py:66
  370.4 5.9 %reshape.68 = bf16[512,2,12,64]{3,2,0,1:T(8,128)(2,1)} reshape(bf16[16,32,2,768]{3,1,0,2:T(8,128)(2,1)} %bitcast.150) | data formatting | bytes 3145728 | tf_op jit(solution)/shard_map/reshape | solution.py:71
  376.3 5.3 %copy.53 = bf16[2,512,12,64]{1,3,2,0:T(8,128)(2,1)} copy(bf16[2,512,12,64]{3,2,1,0:T(8,128)(2,1)} %bitcast.140) | data formatting | bytes 3145728 | tf_op jit(solution)/shard_map/while | solution.py:83
  383.2 3.9 reshape.67
  387.0 5.3 %copy.52 = bf16[2,512,12,64]{1,3,2,0:T(8,128)(2,1)} copy(bf16[2,512,12,64]{3,2,1,0:T(8,128)(2,1)} %bitcast.141) | data formatting | bytes 3145728 | tf_op jit(solution)/shard_map/while | solution.py:83
  393.9 3.9 reshape.66
  397.8 5.5 %copy.51 = bf16[2,512,12,64]{1,3,2,0:T(8,128)(2,1)} copy(bf16[2,512,12,64]{3,2,1,0:T(8,128)(2,1)} %bitcast.142) | data formatting | bytes 3145728 | tf_op jit(solution)/shard_map/while | solution.py:83
  403.2 32.3 %while.10 = (s32[]{:T(128)}, bf16[2,512,12,64]{1,3,2,0:T(8,128)(2,1)S(1)}, bf16[2,512,12,64]{1,3,2,0:T(8,128)(2,1)}, bf16[2,512,12,64]{1,3,2,0:T(8,128)(2,1)}, bf16[2,512,12,64]{1,3,2,0:T(8,128)(2,1)}, /*index=5*/s32[]{:T(128)}) while((s32[]{:T(128)}, bf16[2,512,12,64]{1,3,2,0:T(8,128)(2,1)S(1)}, bf16[2,512,12,64]{1,3,2,0:T(8,128)(2,1)}, ...), condition=%wide.region_10.11_spmd, body=%wide.region_7.10_spmd.sunk | while | flops 821428736 | bytes 28371012 | solution.py:83
  403.2 10.1 %fusion.105 = (f32[12,512]{1,0:T(8,128)S(1)}, f32[12,512,512]{1,2,0:T(8,128)}) fusion(bf16[2,512,12,64]{1,3,2,0:T(8,128)(2,1)} %get-tuple-element.108, s32[]{:T(128)} %get-tuple-element.98, bf16[2,512,12,64]{1,3,2,0:T(8,128)(2,1)} %get-tuple-element.107), kind=kOutput, calls=%fused_computation.82.clone.1 | convolution fusion | flops 412090880 | bytes 14181376 | tf_op jit(solution)/shard_map/while/body/eval_jaxpr/sub | solution.py:78
  413.3 6.0 %fusion.106 = bf16[2,512,12,64]{1,3,2,0:T(8,128)(2,1)S(1)} fusion(bf16[2,512,12,64]{1,3,2,0:T(8,128)(2,1)S(1)} %get-tuple-element.99, s32[]{:T(128)} %get-tuple-element.98, f32[12,512,512]{1,2,0:T(8,128)} %get-tuple-element.90, f32[12,512]{1,0:T(8,128)S(1)} %get-tuple-element.91, bf16[2,512,12,64]{1,3,2,0:T(8,128)(2,1)} %get-tuple-element.106), kind=kOutput, calls=%fused_computation.10.clone.1 | convolution fusion | flops 409337856 | bytes 14189568 | tf_op jit(solution)/shard_map/while/body/eval_jaxpr/hrs,shd->rhd/dot_general | solution.py:79
  419.4 10.1 %fusion.105 = (f32[12,512]{1,0:T(8,128)S(1)}, f32[12,512,512]{1,2,0:T(8,128)}) fusion(bf16[2,512,12,64]{1,3,2,0:T(8,128)(2,1)} %get-tuple-element.108, s32[]{:T(128)} %get-tuple-element.98, bf16[2,512,12,64]{1,3,2,0:T(8,128)(2,1)} %get-tuple-element.107), kind=kOutput, calls=%fused_computation.82.clone.1 | convolution fusion | flops 412090880 | bytes 14181376 | tf_op jit(solution)/shard_map/while/body/eval_jaxpr/sub | solution.py:78
  429.4 6.0 %fusion.106 = bf16[2,512,12,64]{1,3,2,0:T(8,128)(2,1)S(1)} fusion(bf16[2,512,12,64]{1,3,2,0:T(8,128)(2,1)S(1)} %get-tuple-element.99, s32[]{:T(128)} %get-tuple-element.98, f32[12,512,512]{1,2,0:T(8,128)} %get-tuple-element.90, f32[12,512]{1,0:T(8,128)S(1)} %get-tuple-element.91, bf16[2,512,12,64]{1,3,2,0:T(8,128)(2,1)} %get-tuple-element.106), kind=kOutput, calls=%fused_computation.10.clone.1 | convolution fusion | flops 409337856 | bytes 14189568 | tf_op jit(solution)/shard_map/while/body/eval_jaxpr/hrs,shd->rhd/dot_general | solution.py:79
  441.5 26.7 %all_to_all.119 = bf16[512,2,768]{2,1,0:T(2,128)(2,1)S(1)} all-to-all(bf16[512,2,768]{2,1,0:T(2,128)(2,1)S(1)} %copy.55), channel_id=1, replica_groups=mesh['seq'=16,'res'=8] {'seq'}, dimensions={0} | all-to-all | bytes 3145728 | tf_op jit(solution)/shard_map/all_to_all | solution.py:86
  471.6 5.4 %reshape.70 = f32[32,32,768]{2,1,0:T(8,128)} reshape(f32[32,16,2,768]{3,2,1,0:T(2,128)} %copy_bitcast_fusion) | data formatting | bytes 6291456 | tf_op jit(solution)/shard_map/convert_element_type | solution.py:87
  (53 shorter events, 56.1 us)
Async XLA Ops:
  6.5 287.9 %copy-start = (bf16[768,768]{1,0:T(8,128)(2,1)S(1)}, bf16[768,768]{1,0:T(8,128)(2,1)}, u32[]{:S(2)}) copy-start(bf16[768,768]{1,0:T(8,128)(2,1)} %param.15) | copy-start | bytes 3538948
  6.5 2.0 copy-start.2
  6.5 2.6 copy-start.6
  11.7 31.5 %all-to-all-start.1 = ((bf16[32,32,768]{2,1,0:T(8,128)(2,1)}), bf16[32,32,768]{2,1,0:T(8,128)(2,1)}, u32[]{:S(2)}, u32[]{:S(2)}) async-start(bf16[32,32,768]{2,1,0:T(8,128)(2,1)} %convolution_convert_fusion.5), calls=%async_computation.1 | async-start | bytes 3145728 | tf_op jit(solution)/shard_map/all_to_all | solution.py:38
  43.2 26.4 %all-to-all-start.2 = ((bf16[32,32,768]{2,1,0:T(8,128)(2,1)}), bf16[32,32,768]{2,1,0:T(8,128)(2,1)}, u32[]{:S(2)}, u32[]{:S(2)}) async-start(bf16[32,32,768]{2,1,0:T(8,128)(2,1)} %convolution_convert_fusion.4), calls=%async_computation.2 | async-start | bytes 3145728 | tf_op jit(solution)/shard_map/all_to_all | solution.py:39
  47.5 198.0 %all-reduce.2.cloned.1.call-start = ((), (), s32[]{:S(2)}) async-start(), calls=%async_computation.8 | async-start | bytes 6291456 | tf_op jit(solution)/shard_map/psum | solution.py:51
  295.9 3.4 copy-start.3
  296.0 1.8 copy-start.7
  301.3 27.8 %all-to-all-start.6 = ((bf16[32,32,768]{2,0,1:T(8,128)(2,1)}), bf16[32,32,768]{2,0,1:T(8,128)(2,1)S(1)}, u32[]{:S(2)}, u32[]{:S(2)}) async-start(bf16[32,32,768]{2,0,1:T(8,128)(2,1)} %copy.49), calls=%async_computation.6 | async-start | bytes 3145728 | tf_op jit(solution)/shard_map/all_to_all | solution.py:65
  329.1 26.5 %all-to-all-start.5 = ((bf16[32,32,768]{2,0,1:T(8,128)(2,1)}), bf16[32,32,768]{2,0,1:T(8,128)(2,1)}, u32[]{:S(2)}, u32[]{:S(2)}) async-start(bf16[32,32,768]{2,0,1:T(8,128)(2,1)} %copy.47), calls=%async_computation.5 | async-start | bytes 3145728 | tf_op jit(solution)/shard_map/all_to_all | solution.py:64
  355.7 36.7 %all-to-all-start.4 = ((bf16[32,32,768]{2,0,1:T(8,128)(2,1)}), bf16[32,32,768]{2,0,1:T(8,128)(2,1)}, u32[]{:S(2)}, u32[]{:S(2)}) async-start(bf16[32,32,768]{2,0,1:T(8,128)(2,1)} %copy.45), calls=%async_computation.4 | async-start | bytes 3145728 | tf_op jit(solution)/shard_map/all_to_all | solution.py:66
  397.8 5.5 %copy-start.5 = (bf16[2,512,12,64]{1,3,2,0:T(8,128)(2,1)S(1)}, bf16[2,512,12,64]{1,3,2,0:T(8,128)(2,1)}, u32[]{:S(2)}) copy-start(bf16[2,512,12,64]{1,3,2,0:T(8,128)(2,1)} %custom-call) | copy-start | bytes 4718596
  435.5 1.6 copy-start.8
  471.6 5.4 %copy-start.4 = (bf16[32,32,768]{2,1,0:T(8,128)(2,1)S(1)}, bf16[32,32,768]{2,1,0:T(8,128)(2,1)}, u32[]{:S(2)}) copy-start(bf16[32,32,768]{2,1,0:T(8,128)(2,1)} %copy-done.3) | copy-start | bytes 4718596
  477.0 3.6 copy-start.1
Sparse Core Ops, SparseCore 0:
  85.1 160.3 all-reduce.1
where the time goes:
time: 496 us; the launch traced here: 488 us
  waiting for transfers between devices  189 us (38%)
  local copies, waits for them, and re-layouts  81.2 us (16%)
  blocking collectives  79.4 us (16%)
  matrix products  72.8 us (15%)
  starting transfers between devices  37.3 us (8%)
  between operations  13.9 us (3%)
  other arithmetic  13.8 us (3%)
    psum x1, waiting for transfers between devices, on_device(): tied = lax.psum(partial_value, ('seq', 'res'))  124 us
    all_to_all x1, blocking collectives, on_device(): lax.all_to_all(v1, 'res', split_axis=0, concat_axis=1, tiled=True)  26.8 us
    all_to_all x1, blocking collectives, on_device(): lax.all_to_all(colupd, 'seq', split_axis=0, concat_axis=1, tiled=True)  26.7 us
    all_to_all x1, blocking collectives, on_device(): o1 = lax.all_to_all(o_moved, 'res', split_axis=1, concat_axis=0, tiled=True)  25.9 us
    dot_general x8, matrix products, project(): return jnp.dot(inputs, weight, preferred_element_type=jnp.float32)  21.4 us
    sub x2, matrix products, attend(): prob2 = jax.nn.softmax(score, axis=-1).astype(jnp.bfloat16)  20.1 us
    all_to_all x1, waiting for transfers between devices, on_device(): lax.all_to_all(q1, 'res', split_axis=0, concat_axis=1, tiled=True)  19.3 us
    reshape x3, local copies, waits for them, and re-layouts, split_heads(): return field.reshape(field.shape[0], field.shape[1], HEADS, D // HEADS)  17.7 us
  transfers between devices with their start and end apart: 6, of which 5 were waited for; matrix products, arithmetic and copies ran while one was open for 11% of the time, Pallas kernels for 0%

commit v1 on v0

--- a/solution.py
+++ b/solution.py
@@ -48,7 +48,7 @@
         )
         * tied_scale
     )
-    tied = lax.psum(partial_value, ("seq", "res"))
+    tied = lax.psum(lax.psum(partial_value, "res"), "seq")
     prob1 = jax.nn.softmax(tied, axis=-1).astype(jnp.bfloat16)
     o_moved = jnp.einsum(
         "hij,rjhd->rihd", prob1, split_heads(v_moved), preferred_element_type=jnp.float32

time: 496 us -> 614 us (1.24)
  waiting for transfers between devices: 189 us -> 305 us
    psum x1 -> x2, waiting for transfers between devices: 124 us -> 239 us  [on_device(): tied = lax.psum(lax.psum(partial_value, 'res'), 'seq')]
  transfers between devices with their start and end apart: 6 -> 7, of which waited for: 5 -> 6; matrix products, arithmetic and copies ran while one was open for 11% -> 9% of each run, Pallas kernels for 0% -> 0%
where the time goes in v1:
time: 614 us; the launch traced here: 607 us
  waiting for transfers between devices  305 us (50%)
  blocking collectives  83.1 us (14%)
  local copies, waits for them, and re-layouts  81.2 us (13%)
  matrix products  72.8 us (12%)
  starting transfers between devices  37.2 us (6%)
  between operations  13.9 us (2%)
  other arithmetic  13.8 us (2%)
    psum x2, waiting for transfers between devices, on_device(): tied = lax.psum(lax.psum(partial_value, 'res'), 'seq')  239 us
    all_to_all x1, blocking collectives, on_device(): lax.all_to_all(v1, 'res', split_axis=0, concat_axis=1, tiled=True)  29.3 us
    all_to_all x1, blocking collectives, on_device(): o1 = lax.all_to_all(o_moved, 'res', split_axis=1, concat_axis=0, tiled=True)  27 us
    all_to_all x1, blocking collectives, on_device(): lax.all_to_all(colupd, 'seq', split_axis=0, concat_axis=1, tiled=True)  26.7 us
    dot_general x8, matrix products, project(): return jnp.dot(inputs, weight, preferred_element_type=jnp.float32)  21.4 us
    sub x2, matrix products, attend(): prob2 = jax.nn.softmax(score, axis=-1).astype(jnp.bfloat16)  20.1 us
    all_to_all x1, waiting for transfers between devices, on_device(): lax.all_to_all(q1, 'res', split_axis=0, concat_axis=1, tiled=True)  19.3 us
    reshape x3, local copies, waits for them, and re-layouts, split_heads(): return field.reshape(field.shape[0], field.shape[1], HEADS, D // HEADS)  17.7 us
  transfers between devices with their start and end apart: 7, of which 6 were waited for; matrix products, arithmetic and copies ran while one was open for 9% of the time, Pallas kernels for 0%

profile of v1, /device:TPU:1, one launch (start us, length us, event | category | flops | bytes accessed | tf_op | source)
XLA Modules:
  0.0 606.6 jit_solution(15197584632654378315)
XLA Ops:
  11.7 8.3 %all-to-all-start.1 = ((bf16[32,32,768]{2,1,0:T(8,128)(2,1)}), bf16[32,32,768]{2,1,0:T(8,128)(2,1)}, u32[]{:S(2)}, u32[]{:S(2)}) async-start(bf16[32,32,768]{2,1,0:T(8,128)(2,1)} %convolution_convert_fusion.5), calls=%async_computation.1 | async-start | bytes 3145728 | tf_op jit(solution)/shard_map/all_to_all | solution.py:38
  20.1 3.9 convolution_convert_fusion.4
  23.9 19.3 %all-to-all-done.1 = bf16[32,32,768]{2,1,0:T(8,128)(2,1)} async-done(((bf16[32,32,768]{2,1,0:T(8,128)(2,1)}), bf16[32,32,768]{2,1,0:T(8,128)(2,1)}, u32[]{:S(2)}, u32[]{:S(2)}) %all-to-all-start.1) | async-done | bytes 1572896 | tf_op jit(solution)/shard_map/all_to_all | solution.py:38
  43.2 4.3 all-to-all-start.2
  50.3 5.9 reshape.63
  56.2 13.5 %all-to-all-done.2 = bf16[32,32,768]{2,1,0:T(8,128)(2,1)} async-done(((bf16[32,32,768]{2,1,0:T(8,128)(2,1)}), bf16[32,32,768]{2,1,0:T(8,128)(2,1)}, u32[]{:S(2)}, u32[]{:S(2)}) %all-to-all-start.2) | async-done | bytes 1572896 | tf_op jit(solution)/shard_map/all_to_all | solution.py:39
  72.3 5.9 reshape.64
  78.2 6.7 %bitcast_multiply_fusion = f32[12,256,256]{2,1,0:T(8,128)} fusion(bf16[4,256,12,64]{3,2,1,0:T(8,128)(2,1)} %reshape.64, bf16[4,256,12,64]{3,2,1,0:T(8,128)(2,1)} %reshape.63), kind=kOutput, calls=%fused_computation.43 | convolution fusion | flops 403439616 | bytes 6291456 | tf_op jit(solution)/shard_map/rihd,rjhd->hij/dot_general | solution.py:43
  85.0 144.2 %all-reduce.3.cloned.1.call-done = f32[12,256,256]{2,1,0:T(8,128)} async-done(((f32[12,256,256]{2,1,0:T(8,128)}), f32[12,256,256]{2,1,0:T(8,128)}) %all-reduce.3.cloned.1.call-update) | async-done | bytes 3145744 | tf_op jit(solution)/shard_map/psum | solution.py:51
  232.0 29.3 %all_to_all.117 = bf16[32,32,768]{2,1,0:T(8,128)(2,1)S(1)} all-to-all(bf16[32,32,768]{2,1,0:T(8,128)(2,1)S(1)} %convolution_convert_fusion.6), channel_id=1, replica_groups=mesh['seq'=16,'res'=8] {'res'}, dimensions={0} | all-to-all | bytes 3145728 | tf_op jit(solution)/shard_map/all_to_all | solution.py:40
  262.6 5.9 reshape.62
  268.4 94.9 %all-reduce.5.cloned.1.call-done = f32[12,256,256]{2,1,0:T(8,128)} async-done(((f32[12,256,256]{2,1,0:T(8,128)}), f32[12,256,256]{2,1,0:T(8,128)}) %all-reduce.5.cloned.1.call-update) | async-done | bytes 3145744 | tf_op jit(solution)/shard_map/psum | solution.py:51
  367.1 12.5 %fusion.63 = bf16[4,256,12,64]{1,3,0,2:T(8,128)(2,1)} fusion(f32[12,256]{1,0:T(8,128)S(1)} %fusion.92, bf16[4,256,12,64]{3,2,1,0:T(8,128)(2,1)} %reshape.62, f32[12,256,256]{2,1,0:T(8,128)} %all-reduce.5.cloned.1.call-done), kind=kOutput, calls=%fused_computation.68 | convolution fusion | flops 405802240 | bytes 6303744 | tf_op jit(solution)/shard_map/hij,rjhd->rihd/dot_general | solution.py:53
  386.0 27.0 %all_to_all.118 = bf16[4,256,768]{2,0,1:T(4,128)(2,1)S(1)} all-to-all(bf16[4,256,768]{2,0,1:T(4,128)(2,1)} %copy.42), channel_id=1, replica_groups=mesh['seq'=16,'res'=8] {'res'}, dimensions={1} | all-to-all | bytes 3145728 | tf_op jit(solution)/shard_map/all_to_all | solution.py:57
  420.3 6.2 %all-to-all-start.6 = ((bf16[32,32,768]{2,0,1:T(8,128)(2,1)}), bf16[32,32,768]{2,0,1:T(8,128)(2,1)S(1)}, u32[]{:S(2)}, u32[]{:S(2)}) async-start(bf16[32,32,768]{2,0,1:T(8,128)(2,1)} %copy.49), calls=%async_computation.6 | async-start | bytes 3145728 | tf_op jit(solution)/shard_map/all_to_all | solution.py:65
  431.7 16.4 %all-to-all-done.6 = bf16[32,32,768]{2,0,1:T(8,128)(2,1)S(1)} async-done(((bf16[32,32,768]{2,0,1:T(8,128)(2,1)}), bf16[32,32,768]{2,0,1:T(8,128)(2,1)S(1)}, u32[]{:S(2)}, u32[]{:S(2)}) %all-to-all-start.6) | async-done | bytes 1572896 | tf_op jit(solution)/shard_map/all_to_all | solution.py:65
  448.0 4.8 all-to-all-start.5
  458.1 16.4 %all-to-all-done.5 = bf16[32,32,768]{2,0,1:T(8,128)(2,1)} async-done(((bf16[32,32,768]{2,0,1:T(8,128)(2,1)}), bf16[32,32,768]{2,0,1:T(8,128)(2,1)}, u32[]{:S(2)}, u32[]{:S(2)}) %all-to-all-start.5) | async-done | bytes 1572896 | tf_op jit(solution)/shard_map/all_to_all | solution.py:64
  474.6 13.4 %all-to-all-start.4 = ((bf16[32,32,768]{2,0,1:T(8,128)(2,1)}), bf16[32,32,768]{2,0,1:T(8,128)(2,1)}, u32[]{:S(2)}, u32[]{:S(2)}) async-start(bf16[32,32,768]{2,0,1:T(8,128)(2,1)} %copy.45), calls=%async_computation.4 | async-start | bytes 3145728 | tf_op jit(solution)/shard_map/all_to_all | solution.py:66
  489.3 5.9 reshape.68
  495.2 5.3 copy.53
  502.0 3.9 reshape.67
  505.9 5.3 copy.52
  512.8 3.9 reshape.66
  516.6 5.5 copy.51
  522.1 32.3 %while.10 = (s32[]{:T(128)}, bf16[2,512,12,64]{1,3,2,0:T(8,128)(2,1)S(1)}, bf16[2,512,12,64]{1,3,2,0:T(8,128)(2,1)}, bf16[2,512,12,64]{1,3,2,0:T(8,128)(2,1)}, bf16[2,512,12,64]{1,3,2,0:T(8,128)(2,1)}, /*index=5*/s32[]{:T(128)}) while((s32[]{:T(128)}, bf16[2,512,12,64]{1,3,2,0:T(8,128)(2,1)S(1)}, bf16[2,512,12,64]{1,3,2,0:T(8,128)(2,1)}, ...), condition=%wide.region_11.12_spmd, body=%wide.region_8.11_spmd.sunk | while | flops 821428736 | bytes 28371012 | solution.py:83
  522.1 10.1 %fusion.105 = (f32[12,512]{1,0:T(8,128)S(1)}, f32[12,512,512]{1,2,0:T(8,128)}) fusion(bf16[2,512,12,64]{1,3,2,0:T(8,128)(2,1)} %get-tuple-element.108, s32[]{:T(128)} %get-tuple-element.98, bf16[2,512,12,64]{1,3,2,0:T(8,128)(2,1)} %get-tuple-element.107), kind=kOutput, calls=%fused_computation.82.clone.1 | convolution fusion | flops 412090880 | bytes 14181376 | tf_op jit(solution)/shard_map/while/body/eval_jaxpr/sub | solution.py:78
  532.2 6.0 fusion.106
  538.2 10.1 %fusion.105 = (f32[12,512]{1,0:T(8,128)S(1)}, f32[12,512,512]{1,2,0:T(8,128)}) fusion(bf16[2,512,12,64]{1,3,2,0:T(8,128)(2,1)} %get-tuple-element.108, s32[]{:T(128)} %get-tuple-element.98, bf16[2,512,12,64]{1,3,2,0:T(8,128)(2,1)} %get-tuple-element.107), kind=kOutput, calls=%fused_computation.82.clone.1 | convolution fusion | flops 412090880 | bytes 14181376 | tf_op jit(solution)/shard_map/while/body/eval_jaxpr/sub | solution.py:78
  548.3 6.0 fusion.106
  560.4 26.7 %all_to_all.119 = bf16[512,2,768]{2,1,0:T(2,128)(2,1)S(1)} all-to-all(bf16[512,2,768]{2,1,0:T(2,128)(2,1)S(1)} %copy.55), channel_id=1, replica_groups=mesh['seq'=16,'res'=8] {'seq'}, dimensions={0} | all-to-all | bytes 3145728 | tf_op jit(solution)/shard_map/all_to_all | solution.py:86
  590.5 5.4 reshape.70
  (56 shorter events, 59.9 us)
Async XLA Ops:
  6.5 406.9 %copy-start = (bf16[768,768]{1,0:T(8,128)(2,1)S(1)}, bf16[768,768]{1,0:T(8,128)(2,1)}, u32[]{:S(2)}) copy-start(bf16[768,768]{1,0:T(8,128)(2,1)} %param.15) | copy-start | bytes 3538948
  6.5 2.0 copy-start.2
  6.5 2.6 copy-start.6
  11.7 31.5 %all-to-all-start.1 = ((bf16[32,32,768]{2,1,0:T(8,128)(2,1)}), bf16[32,32,768]{2,1,0:T(8,128)(2,1)}, u32[]{:S(2)}, u32[]{:S(2)}) async-start(bf16[32,32,768]{2,1,0:T(8,128)(2,1)} %convolution_convert_fusion.5), calls=%async_computation.1 | async-start | bytes 3145728 | tf_op jit(solution)/shard_map/all_to_all | solution.py:38
  43.2 26.4 %all-to-all-start.2 = ((bf16[32,32,768]{2,1,0:T(8,128)(2,1)}), bf16[32,32,768]{2,1,0:T(8,128)(2,1)}, u32[]{:S(2)}, u32[]{:S(2)}) async-start(bf16[32,32,768]{2,1,0:T(8,128)(2,1)} %convolution_convert_fusion.4), calls=%async_computation.2 | async-start | bytes 3145728 | tf_op jit(solution)/shard_map/all_to_all | solution.py:39
  47.5 181.7 %all-reduce.3.cloned.1.call-start = ((), (), s32[]{:S(2)}) async-start(), calls=%async_computation.8 | async-start | bytes 6291456 | tf_op jit(solution)/shard_map/psum | solution.py:51
  85.0 278.3 %all-reduce.5.cloned.1.call-start = ((), (), s32[]{:S(2)}) async-start(), calls=%async_computation.9 | async-start | bytes 6291456 | tf_op jit(solution)/shard_map/psum | solution.py:51
  414.9 3.3 copy-start.3
  414.9 1.8 copy-start.7
  420.3 27.7 %all-to-all-start.6 = ((bf16[32,32,768]{2,0,1:T(8,128)(2,1)}), bf16[32,32,768]{2,0,1:T(8,128)(2,1)S(1)}, u32[]{:S(2)}, u32[]{:S(2)}) async-start(bf16[32,32,768]{2,0,1:T(8,128)(2,1)} %copy.49), calls=%async_computation.6 | async-start | bytes 3145728 | tf_op jit(solution)/shard_map/all_to_all | solution.py:65
  448.0 26.5 %all-to-all-start.5 = ((bf16[32,32,768]{2,0,1:T(8,128)(2,1)}), bf16[32,32,768]{2,0,1:T(8,128)(2,1)}, u32[]{:S(2)}, u32[]{:S(2)}) async-start(bf16[32,32,768]{2,0,1:T(8,128)(2,1)} %copy.47), calls=%async_computation.5 | async-start | bytes 3145728 | tf_op jit(solution)/shard_map/all_to_all | solution.py:64
  474.6 36.7 %all-to-all-start.4 = ((bf16[32,32,768]{2,0,1:T(8,128)(2,1)}), bf16[32,32,768]{2,0,1:T(8,128)(2,1)}, u32[]{:S(2)}, u32[]{:S(2)}) async-start(bf16[32,32,768]{2,0,1:T(8,128)(2,1)} %copy.45), calls=%async_computation.4 | async-start | bytes 3145728 | tf_op jit(solution)/shard_map/all_to_all | solution.py:66
  516.6 5.5 copy-start.5
  554.4 1.6 copy-start.8
  590.5 5.4 copy-start.4
  595.9 3.6 copy-start.1
Sparse Core Ops, SparseCore 0:
  85.1 144.0 all-reduce.2
  231.7 131.5 all-reduce.4
